TPU v7x, 32 devices: a whole 2x2x4 slice. The times are simulated.
32 devices in a mesh: vocab: 8 (over y, x, core), hid: 4 (over z).
Axes of the slice: x: 2, y: 2, z: 4, core: 2. Of those that a mesh axis runs over, the one named last changes fastest.
Arguments:
- hidden: bfloat16 [1, 1024, 3584], P(None, 'vocab', 'hid'), may hold values from -30 to 30
- unembed: bfloat16 [3584, 81920], P(None, ('vocab', 'hid')), may hold values from -10 to 10
- labels: int32 [1024], P('vocab'), may hold values from 0 to 81919
Outputs:
- token_loss: float32 [1, 1024], replicated
- layer_loss: float32 [1], replicated
All inputs are finite; a program needn't handle non-finite values.
Results may differ from a plain program's by a relative error of at most 0.0003.
Values may be sent and summed in bfloat16 or wider, within the bound.
A program may use at most 128 MiB of HBM per device.

v0:
```python
import jax
import jax.numpy as jnp
from jax import lax
from jax.sharding import PartitionSpec as P


def block_stats(logits, wanted, first_col):
    row_peak = jnp.max(logits, axis=-1)
    row_total = jnp.sum(jnp.exp(logits - row_peak[..., None]), axis=-1)
    columns = first_col + lax.broadcasted_iota(jnp.int32, (1, 1, logits.shape[-1]), 2)
    picked = jnp.sum(jnp.where(wanted[..., None] == columns, logits, 0.0), axis=-1)
    return (row_peak, row_total, picked)


def fold_tokens(layers, weights, first_col):
    vocab_cols = weights.shape[1]

    def add_tokens(held_stats, pieces, offset):
        piece_rows, wanted = pieces
        row_count = piece_rows.shape[1]
        logits = jnp.dot(
            piece_rows.reshape(-1, piece_rows.shape[2]), weights, preferred_element_type=jnp.float32
        )
        part_stats = block_stats(logits.reshape(layers, row_count, vocab_cols), wanted, first_col)
        return tuple((new_value for new_value in part_stats))

    return add_tokens


def body(hidden, unembed, labels):
    layers = hidden.shape[0]
    vocab_cols = unembed.shape[1]
    first_col = lax.axis_index(("vocab", "hid")) * vocab_cols
    targets = labels.reshape(1, -1)
    tokens_all = labels.shape[0] * lax.axis_size("vocab")
    full_rows = lax.all_gather(hidden, "hid", axis=2, tiled=True)
    add_tokens = fold_tokens(layers, unembed, first_col)
    blank_stats = jnp.zeros((layers, tokens_all), jnp.float32)
    row_peak, row_total, picked = add_tokens(
        (blank_stats, blank_stats, blank_stats),
        (
            lax.all_gather(full_rows, "vocab", axis=1, tiled=True),
            lax.all_gather(targets, "vocab", axis=1, tiled=True),
        ),
        jnp.int32(0),
    )
    highest = lax.pmax(row_peak, ("vocab", "hid"))
    row_total, picked = lax.psum(
        (row_total * jnp.exp(row_peak - highest), picked), ("vocab", "hid")
    )
    row_peak = highest
    token_loss = row_peak + jnp.log(row_total) - picked
    return (token_loss, jnp.mean(token_loss, axis=1))


def solution(mesh):
    placed = (P(None, "vocab", "hid"), P(None, ("vocab", "hid")), P("vocab"))
    return jax.shard_map(body, mesh=mesh, in_specs=placed, out_specs=(P(), P()), check_vma=False)
```

profile of v0, /device:TPU:0, one launch (start us, length us, event | category | flops | bytes accessed | tf_op | source)
XLA Modules:
  0.0 201.6 jit_solution(13099708919454776192)
XLA Ops:
  7.2 0.0 all-gather.4.cloned.1.call-start
  7.2 23.5 %all_gather.9 = bf16[1,128,3584]{2,1,0:T(8,128)(2,1)} all-gather(bf16[1,128,896]{2,1,0:T(8,128)(2,1)} %param.3), channel_id=1, replica_groups=mesh['vocab'=8,'hid'=4] {'hid'}, dimensions={2}, use_global_device_ids=true | all-gather | bytes 1146880 | tf_op jit(solution)/shard_map/all_gather | solution.py:36
  30.7 0.0 all-gather.4.cloned.1.call-update
  30.8 8.9 %all-gather.1 = s32[8,1,128]{2,1,0:T(1,128)S(1)} all-gather(s32[1,1,128]{2,1,0:T(1,128)} %bitcast.17), channel_id=2, replica_groups=mesh['vocab'=8,'hid'=4] {'vocab'}, dimensions={0}, use_global_device_ids=true | all-gather | bytes 4608 | tf_op jit(solution)/shard_map/all_gather | solution.py:43
  39.7 40.4 %all-gather.4.cloned.1.call-done = bf16[1,1024,3584]{2,1,0:T(8,128)(2,1)} async-done(((bf16[1,128,3584]{2,1,0:T(8,128)(2,1)}), bf16[1,1024,3584]{2,1,0:T(8,128)(2,1)}) %all-gather.4.cloned.1.call-update) | async-done | bytes 7340048 | tf_op jit(solution)/shard_map/all_gather | solution.py:42
  80.1 25.8 %fusion.3 = (f32[1024]{0:T(1024)S(1)}, f32[1024,2560]{1,0:T(8,128)}) fusion(bf16[3584,2560]{1,0:T(8,128)(2,1)} %param.4, bf16[1,1024,3584]{2,1,0:T(8,128)(2,1)} %all-gather.4.cloned.1.call-done), kind=kOutput, calls=%fused_computation.8 | convolution fusion | flops 18793103360 | bytes 36179968 | tf_op jit(solution)/shard_map/dot_general | solution.py:21
  105.9 39.3 %pmax.7 = f32[1,1024]{1,0:T(1,128)S(1)} all-reduce(f32[1,1024]{1,0:T(1,128)S(1)} %bitcast.12), channel_id=1, replica_groups=mesh['vocab'=8,'hid'=4] {'vocab','hid'}, use_global_device_ids=true, to_apply=%region_1.0 | all-reduce | flops 1024 | bytes 8192 | tf_op jit(solution)/shard_map/pmax | solution.py:47
  145.2 5.5 %exponential_reduce_fusion = (f32[1024]{0:T(1024)S(1)}, f32[1024]{0:T(1024)S(1)}) fusion(f32[1024,2560]{1,0:T(8,128)} %get-tuple-element.9, f32[1024]{0:T(1024)S(1)} %get-tuple-element.8, s32[2560]{0:T(1024)S(1)} %iota_add_fusion, s32[1024]{0:T(1024)S(1)} %bitcast.14), kind=kLoop, calls=%fused_computation.1 | loop fusion | flops 13105152 | bytes 10512384 | tf_op jit(solution)/shard_map/reduce_sum | solution.py:9
  150.7 41.1 %all-reduce = (f32[1,1024]{1,0:T(1,128)S(1)}, f32[1,1024]{1,0:T(1,128)S(1)}) all-reduce(f32[1,1024]{1,0:T(1,128)S(1)} %bitcast.15, f32[1,1024]{1,0:T(1,128)S(1)} %exponential_multiply_fusion), channel_id=1, replica_groups=mesh['vocab'=8,'hid'=4] {'vocab','hid'}, use_global_device_ids=true, to_apply=%region_5.6 | all-reduce | flops 2048 | bytes 16384 | tf_op jit(solution)/shard_map/psum | solution.py:48
  191.7 1.2 fusion.2
  (2 shorter events, 0.0 us)
Async XLA Ops:
  7.2 73.0 %all-gather.4.cloned.1.call-start = ((), (), s32[]{:S(2)}) async-start(), calls=%async_computation | async-start | bytes 8257536 | tf_op jit(solution)/shard_map/all_gather | solution.py:42
Sparse Core Ops, SparseCore 0:
  30.9 49.1 all-gather.3
where the time goes:
time: 202 us
  blocking collectives  113 us (56%)
  waiting for transfers between devices  40.4 us (20%)
  matrix products  25.8 us (13%)
  between operations  15.8 us (8%)
  other arithmetic  6.69 us (3%)
    psum x1, blocking collectives, body(): lax.psum((row_total * jnp.exp(row_peak - highest), picked), ('vocab', 'hi...  41.1 us
    all_gather x1, waiting for transfers between devices, body(): lax.all_gather(full_rows, 'vocab', axis=1, tiled=True)  40.4 us
    pmax x1, blocking collectives, body(): highest = lax.pmax(row_peak, ('vocab', 'hid'))  39.3 us
    dot_general x1, matrix products, add_tokens(): jnp.dot(piece_rows.reshape(-1, piece_rows.shape[2]), weights, preferred_e...  25.8 us
    all_gather x1, blocking collectives, body(): full_rows = lax.all_gather(hidden, 'hid', axis=2, tiled=True)  23.5 us
    all_gather x1, blocking collectives, body(): lax.all_gather(targets, 'vocab', axis=1, tiled=True)  8.92 us
    reduce_sum x1, other arithmetic, block_stats(): row_total = jnp.sum(jnp.exp(logits - row_peak[..., None]), axis=-1)  5.47 us
  transfers between devices with their start and end apart: 1, of which 1 were waited for; matrix products, arithmetic and copies ran while one was open for 0% of the time, Pallas kernels for 0%

commit v1 on v0

--- a/solution.py
+++ b/solution.py
@@ -39,7 +39,7 @@
     row_peak, row_total, picked = add_tokens(
         (blank_stats, blank_stats, blank_stats),
         (
-            lax.all_gather(full_rows, "vocab", axis=1, tiled=True),
+            jnp.concatenate(lax.all_gather(full_rows, "vocab"), axis=1),
             lax.all_gather(targets, "vocab", axis=1, tiled=True),
         ),
         jnp.int32(0),

time: 202 us -> 202 us (level)
  no operation moved by 1% of the time
where the time goes in v1:
time: 202 us
  blocking collectives  113 us (56%)
  waiting for transfers between devices  40.4 us (20%)
  matrix products  25.8 us (13%)
  between operations  15.8 us (8%)
  other arithmetic  6.7 us (3%)
    psum x1, blocking collectives, body(): lax.psum((row_total * jnp.exp(row_peak - highest), picked), ('vocab', 'hi...  41.1 us
    all_gather x1, waiting for transfers between devices, body(): lax.all_gather(full_rows, 'vocab')  40.4 us
    pmax x1, blocking collectives, body(): highest = lax.pmax(row_peak, ('vocab', 'hid'))  39.3 us
    dot_general x1, matrix products, add_tokens(): jnp.dot(piece_rows.reshape(-1, piece_rows.shape[2]), weights, preferred_e...  25.8 us
    all_gather x1, blocking collectives, body(): full_rows = lax.all_gather(hidden, 'hid', axis=2, tiled=True)  23.5 us
    all_gather x1, blocking collectives, body(): lax.all_gather(targets, 'vocab', axis=1, tiled=True)  8.92 us
    reduce_sum x1, other arithmetic, block_stats(): row_total = jnp.sum(jnp.exp(logits - row_peak[..., None]), axis=-1)  5.47 us
  transfers between devices with their start and end apart: 1, of which 1 were waited for; matrix products, arithmetic and copies ran while one was open for 0% of the time, Pallas kernels for 0%

profile of v1, /device:TPU:0, one launch (start us, length us, event | category | flops | bytes accessed | tf_op | source)
XLA Modules:
  0.0 201.6 jit_solution(17848385964768273648)
XLA Ops:
  7.2 0.0 all-gather.5.cloned.1.call-start
  7.2 23.5 %all_gather.12 = bf16[1,128,3584]{2,1,0:T(8,128)(2,1)} all-gather(bf16[1,128,896]{2,1,0:T(8,128)(2,1)} %param.3), channel_id=1, replica_groups=mesh['vocab'=8,'hid'=4] {'hid'}, dimensions={2}, use_global_device_ids=true | all-gather | bytes 1146880 | tf_op jit(solution)/shard_map/all_gather | solution.py:36
  30.7 0.0 all-gather.5.cloned.1.call-update
  30.8 8.9 %all-gather.2 = s32[8,1,128]{2,1,0:T(1,128)S(1)} all-gather(s32[1,1,128]{2,1,0:T(1,128)} %bitcast.14), channel_id=3, replica_groups=mesh['vocab'=8,'hid'=4] {'vocab'}, dimensions={0}, use_global_device_ids=true | all-gather | bytes 4608 | tf_op jit(solution)/shard_map/all_gather | solution.py:43
  39.7 40.4 %all-gather.5.cloned.1.call-done = bf16[8,128,3584]{2,1,0:T(8,128)(2,1)} async-done(((bf16[1,128,3584]{2,1,0:T(8,128)(2,1)}), bf16[8,128,3584]{2,1,0:T(8,128)(2,1)}) %all-gather.5.cloned.1.call-update) | async-done | bytes 7340048 | tf_op jit(solution)/shard_map/all_gather | solution.py:42
  80.1 25.8 %fusion.1 = (f32[1024]{0:T(1024)S(1)}, f32[1024,2560]{1,0:T(8,128)}) fusion(bf16[1024,3584]{1,0:T(8,128)(2,1)} %bitcast.15, bf16[3584,2560]{1,0:T(8,128)(2,1)} %param.4), kind=kOutput, calls=%fused_computation.6 | convolution fusion | flops 18793103360 | bytes 36179968 | tf_op jit(solution)/shard_map/dot_general | solution.py:21
  105.9 39.3 %pmax.7 = f32[1,1024]{1,0:T(1,128)S(1)} all-reduce(f32[1,1024]{1,0:T(1,128)S(1)} %bitcast.9), channel_id=1, replica_groups=mesh['vocab'=8,'hid'=4] {'vocab','hid'}, use_global_device_ids=true, to_apply=%region_1.0 | all-reduce | flops 1024 | bytes 8192 | tf_op jit(solution)/shard_map/pmax | solution.py:47
  145.2 5.5 %exponential_reduce_fusion = (f32[1024]{0:T(1024)S(1)}, f32[1024]{0:T(1024)S(1)}) fusion(f32[1024,2560]{1,0:T(8,128)} %get-tuple-element.9, f32[1024]{0:T(1024)S(1)} %get-tuple-element.8, s32[2560]{0:T(1024)S(1)} %iota_add_fusion, s32[1024]{0:T(1024)S(1)} %bitcast.11), kind=kLoop, calls=%fused_computation.1 | loop fusion | flops 13105152 | bytes 10512384 | tf_op jit(solution)/shard_map/reduce_sum | solution.py:9
  150.7 41.1 %all-reduce = (f32[1,1024]{1,0:T(1,128)S(1)}, f32[1,1024]{1,0:T(1,128)S(1)}) all-reduce(f32[1,1024]{1,0:T(1,128)S(1)} %bitcast.12, f32[1,1024]{1,0:T(1,128)S(1)} %exponential_multiply_fusion), channel_id=1, replica_groups=mesh['vocab'=8,'hid'=4] {'vocab','hid'}, use_global_device_ids=true, to_apply=%region_5.6 | all-reduce | flops 2048 | bytes 16384 | tf_op jit(solution)/shard_map/psum | solution.py:48
  191.7 1.2 fusion
  (2 shorter events, 0.0 us)
Async XLA Ops:
  7.2 73.0 %all-gather.5.cloned.1.call-start = ((), (), s32[]{:S(2)}) async-start(), calls=%async_computation | async-start | bytes 8257536 | tf_op jit(solution)/shard_map/all_gather | solution.py:42
Sparse Core Ops, SparseCore 0:
  30.9 49.1 all-gather.4
